TPU v7x, 512 devices: a whole 4x8x8 slice. The times are simulated.
512 devices in a mesh: row: 16 (over y, core), col: 32 (over x, z).
Axes of the slice: x: 4, y: 8, z: 8, core: 2. Of those that a mesh axis runs over, the one named last changes fastest.
Arguments:
- rhs: bfloat16 [4, 16, 32, 64, 256], P(None, 'row', 'col'), may hold values from -6 to 6
- dinv: float32 [4, 16, 32, 64, 64], P(None, 'row', 'col'), may hold values from -1.5 to 1.5, as said below
- lower: bfloat16 [6, 16, 32, 32, 64, 128], P(None, 'row', 'col'), may hold values from -0.0625 to 0.0625
- sources: int32 [6, 16, 32, 32, 2], P(None, 'row', 'col'), may hold values from -1 to 15, as said below
Outputs:
- solution: float32 [4, 16, 32, 64, 256], P(None, 'row', 'col')
Inputs may be any that keep to these rules, and one draw needn't show every extreme that they name: `dinv`: lower triangular. `sources`: for each level pair, holder and target, the live entries are distinct; in every level pair every device has a target with all 2 entries live.
All inputs are finite; a program needn't handle non-finite values.
Results may differ from a plain program's by a relative error of at most 0.002.
Values may be sent and summed in bfloat16 or wider, within the bound.
No kernel may reach another device: no remote copies, remote signals or barrier semaphores. Data moves between devices by JAX's collectives and lax.ppermute only.
A program may use at most 64 MiB of HBM per device.

v0:
```python
import jax
import jax.numpy as jnp
from jax import lax
from jax.sharding import PartitionSpec as P


def level_terms(blocks, indices, gathered):
    clipped = jnp.maximum(indices, 0)
    picked = jnp.take(gathered, clipped, axis=0)
    picked = jnp.where((indices >= 0)[:, :, None, None], picked, jnp.zeros((), gathered.dtype))
    peer_count, per_count, block_rows, rhs_width = picked.shape
    picked = picked.reshape(peer_count, per_count * block_rows, rhs_width)
    return jnp.einsum("qik,qkn->qin", blocks, picked, preferred_element_type=jnp.float32)


def on_device(rhs, dinv, lower, sources):
    levels = rhs.shape[0]
    pair_of = {}
    for section in range(levels):
        for target in range(section + 1, levels):
            pair_of[section, target] = len(pair_of)
    gathered = []
    results = []
    for section in range(levels):
        residual = rhs[section, 0, 0].astype(jnp.float32)
        if section:
            partial = None
            for earlier in range(section):
                pair = pair_of[earlier, section]
                term = level_terms(lower[pair, 0, 0], sources[pair, 0, 0], gathered[earlier])
                partial = term if partial is None else partial + term
            arrived = lax.all_to_all(
                partial.astype(jnp.bfloat16), "col", split_axis=0, concat_axis=0, tiled=True
            )
            residual = residual - jnp.sum(arrived.astype(jnp.float32), axis=0)
        solution = jnp.dot(
            dinv[section, 0, 0],
            residual,
            precision=lax.Precision.HIGHEST,
            preferred_element_type=jnp.float32,
        )
        results.append(solution)
        if section + 1 < levels:
            solved = solution.astype(jnp.bfloat16)
            gathered.append(lax.all_gather(solved[None], "row", axis=0, tiled=True))
    return jnp.stack(results)[:, None, None]


def solution(mesh):
    in_specs = (
        P(None, "row", "col", None, None),
        P(None, "row", "col", None, None),
        P(None, "row", "col", None, None, None),
        P(None, "row", "col", None, None),
    )
    out_specs = P(None, "row", "col", None, None)
    return jax.shard_map(
        on_device, mesh=mesh, in_specs=in_specs, out_specs=out_specs, check_vma=False
    )
```

profile of v0, /device:TPU:8, one launch (start us, length us, event | category | flops | bytes accessed | tf_op | source)
XLA Modules:
  0.0 183.5 jit_solution(16684669490472690284)
XLA Ops:
  0.0 1.3 compare_and_fusion.1
  1.3 1.4 compare_bitcast_fusion.1
  2.7 0.1 copy.26
  2.8 0.1 reshape.152
  2.9 0.9 fusion.40
  3.8 21.4 %all-gather = bf16[1024,256]{1,0:T(8,128)(2,1)S(1)} all-gather(bf16[64,256]{1,0:T(8,128)(2,1)S(1)} %get-tuple-element.34), channel_id=2, replica_groups=mesh['row'=16,'col'=32] {'row'}, dimensions={0}, use_global_device_ids=true | all-gather | bytes 557056 | tf_op jit(solution)/shard_map/all_gather | solution.py:45
  25.2 0.1 copy.25
  25.3 0.1 copy.24
  25.4 0.7 gather_fusion
  26.1 0.3 select_select_fusion.5
  26.5 2.5 %fusion = bf16[32,64,256]{2,1,0:T(8,128)(2,1)} fusion(bf16[32,128,256]{2,1,0:T(8,128)(2,1)S(1)} %bitcast.153, bf16[6,1,1,32,64,128]{5,4,3,2,1,0:T(8,128)(2,1)} %param.8), kind=kOutput, calls=%fused_computation.18 | convolution fusion | flops 134742016 | bytes 3670016 | tf_op jit(solution)/shard_map/qik,qkn->qin/dot_general | solution.py:13
  28.9 9.5 %all-to-all-start = ((bf16[32,64,256]{2,1,0:T(8,128)(2,1)}), bf16[32,64,256]{2,1,0:T(8,128)(2,1)}, u32[]{:S(2)}, u32[]{:S(2)}) async-start(bf16[32,64,256]{2,1,0:T(8,128)(2,1)} %fusion), calls=%async_computation | async-start | bytes 2097152 | tf_op jit(solution)/shard_map/all_to_all | solution.py:32
  38.5 0.1 copy.32
  38.5 0.1 reshape.160
  38.7 0.1 copy.31
  38.8 0.1 copy.30
  38.9 0.1 copy.29
  38.9 0.1 reshape.156
  39.1 0.7 gather_fusion.1
  39.8 0.1 copy.28
  39.9 0.1 copy.27
  40.0 0.3 select_select_fusion.4
  40.3 2.9 %fusion.9 = f32[32,256,64]{1,2,0:T(8,128)} fusion(bf16[32,128,256]{2,1,0:T(8,128)(2,1)S(1)} %bitcast.159, bf16[6,1,1,32,64,128]{5,4,3,2,1,0:T(8,128)(2,1)} %param.8), kind=kOutput, calls=%fused_computation.28 | convolution fusion | flops 134217728 | bytes 4718592 | tf_op jit(solution)/shard_map/qik,qkn->qin/dot_general | solution.py:13
  43.2 24.3 %all-to-all-done = bf16[32,64,256]{2,1,0:T(8,128)(2,1)} async-done(((bf16[32,64,256]{2,1,0:T(8,128)(2,1)}), bf16[32,64,256]{2,1,0:T(8,128)(2,1)}, u32[]{:S(2)}, u32[]{:S(2)}) %all-to-all-start) | async-done | bytes 1048608 | tf_op jit(solution)/shard_map/all_to_all | solution.py:32
  67.5 1.4 convert_reduce_fusion.2
  68.9 0.2 bitcast_convert_fusion.1
  69.2 17.4 %all-gather.1 = bf16[1024,256]{1,0:T(8,128)(2,1)S(1)} all-gather(bf16[64,256]{1,0:T(8,128)(2,1)S(1)} %get-tuple-element.36), channel_id=3, replica_groups=mesh['row'=16,'col'=32] {'row'}, dimensions={0}, use_global_device_ids=true | all-gather | bytes 557056 | tf_op jit(solution)/shard_map/all_gather | solution.py:45
  86.6 0.7 gather_fusion.2
  87.3 0.3 select_select_fusion.3
  87.6 1.2 copy-done.2
  88.9 2.6 %fusion.1 = bf16[32,64,256]{2,1,0:T(8,128)(2,1)} fusion(f32[32,256,64]{1,2,0:T(8,128)S(1)} %copy-done.2, bf16[32,128,256]{2,1,0:T(8,128)(2,1)S(1)} %bitcast.164, bf16[6,1,1,32,64,128]{5,4,3,2,1,0:T(8,128)(2,1)} %param.8), kind=kOutput, calls=%fused_computation.19 | convolution fusion | flops 135266304 | bytes 5767168 | tf_op jit(solution)/shard_map/qik,qkn->qin/dot_general | solution.py:13
  91.5 5.2 %all-to-all-start.1 = ((bf16[32,64,256]{2,1,0:T(8,128)(2,1)}), bf16[32,64,256]{2,1,0:T(8,128)(2,1)}, u32[]{:S(2)}, u32[]{:S(2)}) async-start(bf16[32,64,256]{2,1,0:T(8,128)(2,1)} %fusion.1), calls=%async_computation.1 | async-start | bytes 2097152 | tf_op jit(solution)/shard_map/all_to_all | solution.py:32
  96.8 0.1 copy.41
  96.8 0.7 reshape.172
  97.5 0.1 copy.40
  97.6 0.1 copy.39
  97.8 0.1 copy.38
  97.8 0.6 reshape.168
  98.5 0.1 copy.37
  98.6 0.7 copy.36
  99.4 0.1 reshape.164
  99.5 0.7 gather_fusion.3
  100.2 0.7 copy.34
  100.9 0.8 copy.33
  101.6 0.7 pad_clamp_fusion
  102.3 0.6 pad_clamp_fusion.1
  102.9 0.3 select_select_fusion.2
  103.3 2.8 %fusion.6 = f32[32,256,64]{1,2,0:T(8,128)} fusion(bf16[32,128,256]{2,1,0:T(8,128)(2,1)S(1)} %bitcast.161, bf16[6,1,1,32,64,128]{5,4,3,2,1,0:T(8,128)(2,1)} %param.8), kind=kOutput, calls=%fused_computation.25 | convolution fusion | flops 134217728 | bytes 4718592 | tf_op jit(solution)/shard_map/qik,qkn->qin/dot_general | solution.py:13
  106.1 0.7 gather_fusion.4
  106.8 0.3 select_select_fusion.1
  107.1 2.8 %fusion.4 = f32[32,256,64]{1,2,0:T(8,128)} fusion(bf16[32,128,256]{2,1,0:T(8,128)(2,1)S(1)} %bitcast.162, bf16[6,1,1,32,64,128]{5,4,3,2,1,0:T(8,128)(2,1)} %param.8), kind=kOutput, calls=%fused_computation.23 | convolution fusion | flops 134217728 | bytes 4718592 | tf_op jit(solution)/shard_map/qik,qkn->qin/dot_general | solution.py:13
  110.0 15.9 %all-to-all-done.1 = bf16[32,64,256]{2,1,0:T(8,128)(2,1)} async-done(((bf16[32,64,256]{2,1,0:T(8,128)(2,1)}), bf16[32,64,256]{2,1,0:T(8,128)(2,1)}, u32[]{:S(2)}, u32[]{:S(2)}) %all-to-all-start.1) | async-done | bytes 1048608 | tf_op jit(solution)/shard_map/all_to_all | solution.py:32
  125.8 1.4 convert_reduce_fusion.1
  127.2 0.2 bitcast_convert_fusion
  127.4 16.4 %all-gather.2 = bf16[1024,256]{1,0:T(8,128)(2,1)S(1)} all-gather(bf16[64,256]{1,0:T(8,128)(2,1)S(1)} %get-tuple-element.38), channel_id=4, replica_groups=mesh['row'=16,'col'=32] {'row'}, dimensions={0}, use_global_device_ids=true | all-gather | bytes 557056 | tf_op jit(solution)/shard_map/all_gather | solution.py:45
  143.8 0.7 gather_fusion.5
  144.5 0.3 select_select_fusion
  144.8 1.2 copy-done
  146.1 0.6 copy-done.1
  146.7 1.7 fusion.2
  148.4 34.0 %all_to_all.15 = bf16[32,64,256]{2,1,0:T(8,128)(2,1)S(1)} all-to-all(bf16[32,64,256]{2,1,0:T(8,128)(2,1)S(1)} %fusion.2), channel_id=1, replica_groups=mesh['row'=16,'col'=32] {'col'}, dimensions={0} | all-to-all | bytes 2097152 | tf_op jit(solution)/shard_map/all_to_all | solution.py:32
  182.4 0.2 convert_reduce_fusion
  182.6 0.2 convolution_bitcast_fusion
  182.8 0.7 maximum_bitcast_fusion
  (26 shorter events, 0.2 us)
Async XLA Ops:
  28.9 38.6 %all-to-all-start = ((bf16[32,64,256]{2,1,0:T(8,128)(2,1)}), bf16[32,64,256]{2,1,0:T(8,128)(2,1)}, u32[]{:S(2)}, u32[]{:S(2)}) async-start(bf16[32,64,256]{2,1,0:T(8,128)(2,1)} %fusion), calls=%async_computation | async-start | bytes 2097152 | tf_op jit(solution)/shard_map/all_to_all | solution.py:32
  40.3 28.6 %copy-start.3 = (f32[4,1,1,64,64]{4,3,2,1,0:T(8,128)S(1)}, f32[4,1,1,64,64]{4,3,2,1,0:T(8,128)}, u32[]{:S(2)}) copy-start(f32[4,1,1,64,64]{4,3,2,1,0:T(8,128)} %param.7) | copy-start | bytes 196612
  40.3 28.6 %copy-start.4 = (bf16[4,1,1,64,256]{4,3,2,1,0:T(8,128)(2,1)S(1)}, bf16[4,1,1,64,256]{4,3,2,1,0:T(8,128)(2,1)}, u32[]{:S(2)}) copy-start(bf16[4,1,1,64,256]{4,3,2,1,0:T(8,128)(2,1)} %param.6) | copy-start | bytes 393220
  87.3 1.6 copy-start.2
  91.5 5.3 %copy-start.7 = (s32[32,2]{0,1:T(2,128)S(1)}, s32[32,2]{0,1:T(2,128)}, u32[]{:S(2)}) copy-start(s32[32,2]{0,1:T(2,128)} %get-tuple-element.33) | copy-start | bytes 772
  91.5 6.1 %copy-start.9 = (pred[32,2]{0,1:T(4,128)(4,1)S(1)}, pred[32,2]{0,1:T(4,128)(4,1)}, u32[]{:S(2)}) copy-start(pred[32,2]{0,1:T(4,128)(4,1)} %get-tuple-element.32) | copy-start | bytes 196
  91.5 6.2 %copy-start.11 = (pred[32,2]{0,1:T(4,128)(4,1)S(1)}, pred[32,2]{0,1:T(4,128)(4,1)}, u32[]{:S(2)}) copy-start(pred[32,2]{0,1:T(4,128)(4,1)} %get-tuple-element.23) | copy-start | bytes 196
  91.5 7.0 %copy-start.8 = (pred[32,2]{0,1:T(4,128)(4,1)S(1)}, pred[32,2]{0,1:T(4,128)(4,1)}, u32[]{:S(2)}) copy-start(pred[32,2]{0,1:T(4,128)(4,1)} %get-tuple-element.6) | copy-start | bytes 196
  91.5 7.1 %copy-start.10 = (pred[32,2]{0,1:T(4,128)(4,1)S(1)}, pred[32,2]{0,1:T(4,128)(4,1)}, u32[]{:S(2)}) copy-start(pred[32,2]{0,1:T(4,128)(4,1)} %get-tuple-element.18) | copy-start | bytes 196
  91.5 7.8 %copy-start.6 = (s32[32,2]{0,1:T(2,128)S(1)}, s32[32,2]{0,1:T(2,128)}, u32[]{:S(2)}) copy-start(s32[32,2]{0,1:T(2,128)} %get-tuple-element.31) | copy-start | bytes 772
  91.5 34.3 %all-to-all-start.1 = ((bf16[32,64,256]{2,1,0:T(8,128)(2,1)}), bf16[32,64,256]{2,1,0:T(8,128)(2,1)}, u32[]{:S(2)}, u32[]{:S(2)}) async-start(bf16[32,64,256]{2,1,0:T(8,128)(2,1)} %fusion.1), calls=%async_computation.1 | async-start | bytes 2097152 | tf_op jit(solution)/shard_map/all_to_all | solution.py:32
  106.1 0.7 copy-start.5
  144.5 1.6 copy-start
  144.5 2.2 %copy-start.1 = (f32[32,256,64]{1,2,0:T(8,128)S(1)}, f32[32,256,64]{1,2,0:T(8,128)}, u32[]{:S(2)}) copy-start(f32[32,256,64]{1,2,0:T(8,128)} %fusion.4) | copy-start | bytes 6291460
where the time goes:
time: 184 us; the launch traced here: 183 us
  blocking collectives  89.2 us (48%)
  waiting for transfers between devices  40.2 us (22%)
  matrix products  16.8 us (9%)
  starting transfers between devices  14.7 us (8%)
  local copies, waits for them, and re-layouts  12.6 us (7%)
  other arithmetic  9.61 us (5%)
    all_gather x3, blocking collectives, on_device(): gathered.append(lax.all_gather(solved[None], 'row', axis=0, tiled=True))  55.2 us
    all_to_all x2, waiting for transfers between devices, on_device(): lax.all_to_all(partial.astype(jnp.bfloat16), 'col', split_axis=0, concat_...  40.2 us
    all_to_all x1, blocking collectives, on_device(): lax.all_to_all(partial.astype(jnp.bfloat16), 'col', split_axis=0, concat_...  34 us
    dot_general x6, matrix products, level_terms(): jnp.einsum('qik,qkn->qin', blocks, picked, preferred_element_type=jnp.flo...  15.3 us
    all_to_all x2, starting transfers between devices, on_device(): lax.all_to_all(partial.astype(jnp.bfloat16), 'col', split_axis=0, concat_...  14.7 us
    gather x6, local copies, waits for them, and re-layouts, level_terms(): picked = jnp.take(gathered, clipped, axis=0)  4.08 us
  transfers between devices with their start and end apart: 2, of which 2 were waited for; matrix products, arithmetic and copies ran while one was open for 10% of the time, Pallas kernels for 0%

commit v1 on v0

--- a/solution.py
+++ b/solution.py
@@ -2,6 +2,19 @@
 import jax.numpy as jnp
 from jax import lax
 from jax.sharding import PartitionSpec as P
+
+
+def gather_around(x, axis, dim):
+    ways = lax.axis_size(axis)
+    up = [(d, (d + 1) % ways) for d in range(ways)]
+    down = [(d, (d - 1) % ways) for d in range(ways)]
+    earlier, later = ([x], [x])
+    for _ in range(ways // 2):
+        earlier.append(lax.ppermute(earlier[-1], axis, up))
+    for _ in range((ways - 1) // 2):
+        later.append(lax.ppermute(later[-1], axis, down))
+    line = jnp.concatenate([*earlier[::-1], *later[1:]], axis=dim)
+    return jnp.roll(line, (lax.axis_index(axis) - ways // 2) * x.shape[dim], axis=dim)
 
 
 def level_terms(blocks, indices, gathered):
@@ -42,7 +55,7 @@
         results.append(solution)
         if section + 1 < levels:
             solved = solution.astype(jnp.bfloat16)
-            gathered.append(lax.all_gather(solved[None], "row", axis=0, tiled=True))
+            gathered.append(gather_around(solved[None], "row", 0))
     return jnp.stack(results)[:, None, None]
 
 

time: 184 us -> 243 us (1.32)
  the two profiles are of different devices: /device:TPU:8 before, /device:TPU:25 now
where the time goes in v1:
time: 243 us; the launch traced here: 242 us
  blocking collectives  101 us (42%)
  starting transfers between devices  73.6 us (30%)
  waiting for transfers between devices  27.6 us (11%)
  matrix products  17 us (7%)
  local copies, waits for them, and re-layouts  15 us (6%)
  other arithmetic  7.17 us (3%)
    all_to_all x3, blocking collectives, on_device(): lax.all_to_all(partial.astype(jnp.bfloat16), 'col', split_axis=0, concat_...  101 us
    ppermute x24, starting transfers between devices, gather_around(): earlier.append(lax.ppermute(earlier[-1], axis, up))  73.5 us
    ppermute x21, waiting for transfers between devices, gather_around(): later.append(lax.ppermute(later[-1], axis, down))  15.1 us
    dot_general x6, matrix products, level_terms(): jnp.einsum('qik,qkn->qin', blocks, picked, preferred_element_type=jnp.flo...  13.2 us
    ppermute x24, waiting for transfers between devices, gather_around(): earlier.append(lax.ppermute(earlier[-1], axis, up))  12.6 us
    unnamed x72, local copies, waits for them, and re-layouts  5.64 us
  transfers between devices with their start and end apart: 45, of which 20 were waited for; matrix products, arithmetic and copies ran while one was open for 9% of the time, Pallas kernels for 0%

profile of v1, /device:TPU:25, one launch (start us, length us, event | category | flops | bytes accessed | tf_op | source)
XLA Modules:
  0.0 242.2 jit_solution(10992955940204131690)
XLA Ops:
  0.0 0.9 fusion.34
  1.0 3.1 %collective-permute-start = (bf16[1,64,256]{2,1,0:T(8,128)(2,1)S(1)}, bf16[1,64,256]{2,1,0:T(8,128)(2,1)S(1)}, u32[]{:S(2)}, u32[]{:S(2)}) collective-permute-start(bf16[1,64,256]{2,1,0:T(8,128)(2,1)S(1)} %convert_bitcast_fusion), channel_id=1, source_target_pairs={{0,32},{32,64},{64,96},{96,128},{128,160},{160,192},{192,224},{224... | collective-permute-start | bytes 98312 | tf_op jit(solution)/shard_map/ppermute | solution.py:13
  4.0 1.0 collective-permute-done
  5.1 3.6 %collective-permute-start.1 = (bf16[1,64,256]{2,1,0:T(8,128)(2,1)S(1)}, bf16[1,64,256]{2,1,0:T(8,128)(2,1)S(1)}, u32[]{:S(2)}, u32[]{:S(2)}) collective-permute-start(bf16[1,64,256]{2,1,0:T(8,128)(2,1)S(1)} %collective-permute-done), channel_id=1, source_target_pairs={{0,32},{32,64},{64,96},{96,128},{128,160},{160,192},{192,224},{224... | collective-permute-start | bytes 98312 | tf_op jit(solution)/shard_map/ppermute | solution.py:13
  8.6 1.0 collective-permute-done.1
  9.7 3.5 %collective-permute-start.2 = (bf16[1,64,256]{2,1,0:T(8,128)(2,1)S(1)}, bf16[1,64,256]{2,1,0:T(8,128)(2,1)S(1)}, u32[]{:S(2)}, u32[]{:S(2)}) collective-permute-start(bf16[1,64,256]{2,1,0:T(8,128)(2,1)S(1)} %collective-permute-done.1), channel_id=1, source_target_pairs={{0,32},{32,64},{64,96},{96,128},{128,160},{160,192},{192,224},{224... | collective-permute-start | bytes 98312 | tf_op jit(solution)/shard_map/ppermute | solution.py:13
  13.2 1.0 collective-permute-done.2
  14.2 3.5 %collective-permute-start.3 = (bf16[1,64,256]{2,1,0:T(8,128)(2,1)S(1)}, bf16[1,64,256]{2,1,0:T(8,128)(2,1)S(1)}, u32[]{:S(2)}, u32[]{:S(2)}) collective-permute-start(bf16[1,64,256]{2,1,0:T(8,128)(2,1)S(1)} %collective-permute-done.2), channel_id=1, source_target_pairs={{0,32},{32,64},{64,96},{96,128},{128,160},{160,192},{192,224},{224... | collective-permute-start | bytes 98312 | tf_op jit(solution)/shard_map/ppermute | solution.py:13
  17.7 1.0 collective-permute-done.3
  18.8 3.5 %collective-permute-start.4 = (bf16[1,64,256]{2,1,0:T(8,128)(2,1)S(1)}, bf16[1,64,256]{2,1,0:T(8,128)(2,1)S(1)}, u32[]{:S(2)}, u32[]{:S(2)}) collective-permute-start(bf16[1,64,256]{2,1,0:T(8,128)(2,1)S(1)} %collective-permute-done.3), channel_id=1, source_target_pairs={{0,32},{32,64},{64,96},{96,128},{128,160},{160,192},{192,224},{224... | collective-permute-start | bytes 98312 | tf_op jit(solution)/shard_map/ppermute | solution.py:13
  22.3 1.0 collective-permute-done.4
  23.3 3.5 %collective-permute-start.5 = (bf16[1,64,256]{2,1,0:T(8,128)(2,1)S(1)}, bf16[1,64,256]{2,1,0:T(8,128)(2,1)S(1)}, u32[]{:S(2)}, u32[]{:S(2)}) collective-permute-start(bf16[1,64,256]{2,1,0:T(8,128)(2,1)S(1)} %collective-permute-done.4), channel_id=1, source_target_pairs={{0,32},{32,64},{64,96},{96,128},{128,160},{160,192},{192,224},{224... | collective-permute-start | bytes 98312 | tf_op jit(solution)/shard_map/ppermute | solution.py:13
  26.8 1.3 compare_and_fusion.1
  28.2 3.2 %collective-permute-start.6 = (bf16[1,64,256]{2,1,0:T(8,128)(2,1)S(1)}, bf16[1,64,256]{2,1,0:T(8,128)(2,1)S(1)}, u32[]{:S(2)}, u32[]{:S(2)}) collective-permute-start(bf16[1,64,256]{2,1,0:T(8,128)(2,1)S(1)} %collective-permute-done.5), channel_id=1, source_target_pairs={{0,32},{32,64},{64,96},{96,128},{128,160},{160,192},{192,224},{224... | collective-permute-start | bytes 98312 | tf_op jit(solution)/shard_map/ppermute | solution.py:13
  31.4 1.4 compare_bitcast_fusion.1
  33.0 3.0 %collective-permute-start.7 = (bf16[1,64,256]{2,1,0:T(8,128)(2,1)S(1)}, bf16[1,64,256]{2,1,0:T(8,128)(2,1)S(1)}, u32[]{:S(2)}, u32[]{:S(2)}) collective-permute-start(bf16[1,64,256]{2,1,0:T(8,128)(2,1)S(1)} %collective-permute-done.6), channel_id=1, source_target_pairs={{0,32},{32,64},{64,96},{96,128},{128,160},{160,192},{192,224},{224... | collective-permute-start | bytes 98312 | tf_op jit(solution)/shard_map/ppermute | solution.py:13
  36.1 1.4 collective-permute-done.13
  37.7 4.4 %collective-permute-done.14 = bf16[1,64,256]{2,1,0:T(8,128)(2,1)S(1)} collective-permute-done((bf16[1,64,256]{2,1,0:T(8,128)(2,1)S(1)}, bf16[1,64,256]{2,1,0:T(8,128)(2,1)S(1)}, u32[]{:S(2)}, u32[]{:S(2)}) %collective-permute-start.14) | collective-permute-done | bytes 32800 | tf_op jit(solution)/shard_map/ppermute | solution.py:15
  43.3 1.5 fusion
  44.8 39.1 %all_to_all.15 = bf16[32,64,256]{2,1,0:T(8,128)(2,1)S(1)} all-to-all(bf16[32,64,256]{2,1,0:T(8,128)(2,1)S(1)} %fusion), channel_id=1, replica_groups=mesh['row'=16,'col'=32] {'col'}, dimensions={0} | all-to-all | bytes 2097152 | tf_op jit(solution)/shard_map/all_to_all | solution.py:45
  84.1 1.0 fusion.24
  85.1 1.2 collective-permute-done.15
  86.3 3.3 %collective-permute-start.16 = (bf16[1,64,256]{2,1,0:T(8,128)(2,1)S(1)}, bf16[1,64,256]{2,1,0:T(8,128)(2,1)S(1)}, u32[]{:S(2)}, u32[]{:S(2)}) collective-permute-start(bf16[1,64,256]{2,1,0:T(8,128)(2,1)S(1)} %collective-permute-done.15), channel_id=1, source_target_pairs={{0,32},{32,64},{64,96},{96,128},{128,160},{160,192},{192,224},{224... | collective-permute-start | bytes 98312 | tf_op jit(solution)/shard_map/ppermute | solution.py:13
  89.6 1.0 collective-permute-done.16
  90.7 3.5 %collective-permute-start.17 = (bf16[1,64,256]{2,1,0:T(8,128)(2,1)S(1)}, bf16[1,64,256]{2,1,0:T(8,128)(2,1)S(1)}, u32[]{:S(2)}, u32[]{:S(2)}) collective-permute-start(bf16[1,64,256]{2,1,0:T(8,128)(2,1)S(1)} %collective-permute-done.16), channel_id=1, source_target_pairs={{0,32},{32,64},{64,96},{96,128},{128,160},{160,192},{192,224},{224... | collective-permute-start | bytes 98312 | tf_op jit(solution)/shard_map/ppermute | solution.py:13
  94.2 1.0 collective-permute-done.17
  95.2 3.5 %collective-permute-start.18 = (bf16[1,64,256]{2,1,0:T(8,128)(2,1)S(1)}, bf16[1,64,256]{2,1,0:T(8,128)(2,1)S(1)}, u32[]{:S(2)}, u32[]{:S(2)}) collective-permute-start(bf16[1,64,256]{2,1,0:T(8,128)(2,1)S(1)} %collective-permute-done.17), channel_id=1, source_target_pairs={{0,32},{32,64},{64,96},{96,128},{128,160},{160,192},{192,224},{224... | collective-permute-start | bytes 98312 | tf_op jit(solution)/shard_map/ppermute | solution.py:13
  99.8 3.5 %collective-permute-start.19 = (bf16[1,64,256]{2,1,0:T(8,128)(2,1)S(1)}, bf16[1,64,256]{2,1,0:T(8,128)(2,1)S(1)}, u32[]{:S(2)}, u32[]{:S(2)}) collective-permute-start(bf16[1,64,256]{2,1,0:T(8,128)(2,1)S(1)} %collective-permute-done.18), channel_id=1, source_target_pairs={{0,32},{32,64},{64,96},{96,128},{128,160},{160,192},{192,224},{224... | collective-permute-start | bytes 98312 | tf_op jit(solution)/shard_map/ppermute | solution.py:13
  104.3 3.5 %collective-permute-start.20 = (bf16[1,64,256]{2,1,0:T(8,128)(2,1)S(1)}, bf16[1,64,256]{2,1,0:T(8,128)(2,1)S(1)}, u32[]{:S(2)}, u32[]{:S(2)}) collective-permute-start(bf16[1,64,256]{2,1,0:T(8,128)(2,1)S(1)} %collective-permute-done.19), channel_id=1, source_target_pairs={{0,32},{32,64},{64,96},{96,128},{128,160},{160,192},{192,224},{224... | collective-permute-start | bytes 98312 | tf_op jit(solution)/shard_map/ppermute | solution.py:13
  109.0 3.4 %collective-permute-start.21 = (bf16[1,64,256]{2,1,0:T(8,128)(2,1)S(1)}, bf16[1,64,256]{2,1,0:T(8,128)(2,1)S(1)}, u32[]{:S(2)}, u32[]{:S(2)}) collective-permute-start(bf16[1,64,256]{2,1,0:T(8,128)(2,1)S(1)} %collective-permute-done.20), channel_id=1, source_target_pairs={{0,32},{32,64},{64,96},{96,128},{128,160},{160,192},{192,224},{224... | collective-permute-start | bytes 98312 | tf_op jit(solution)/shard_map/ppermute | solution.py:13
  112.7 0.8 collective-permute-done.27
  113.5 3.4 %collective-permute-start.22 = (bf16[1,64,256]{2,1,0:T(8,128)(2,1)S(1)}, bf16[1,64,256]{2,1,0:T(8,128)(2,1)S(1)}, u32[]{:S(2)}, u32[]{:S(2)}) collective-permute-start(bf16[1,64,256]{2,1,0:T(8,128)(2,1)S(1)} %collective-permute-done.21), channel_id=1, source_target_pairs={{0,32},{32,64},{64,96},{96,128},{128,160},{160,192},{192,224},{224... | collective-permute-start | bytes 98312 | tf_op jit(solution)/shard_map/ppermute | solution.py:13
  117.0 2.8 %fusion.12 = f32[32,256,64]{1,2,0:T(8,128)} fusion(bf16[32,128,256]{2,1,0:T(8,128)(2,1)S(1)} %bitcast.152, bf16[6,1,1,32,64,128]{5,4,3,2,1,0:T(8,128)(2,1)} %param.10), kind=kOutput, calls=%fused_computation.37 | convolution fusion | flops 134217728 | bytes 4718592 | tf_op jit(solution)/shard_map/qik,qkn->qin/dot_general | solution.py:26
  120.0 4.4 %collective-permute-done.29 = bf16[1,64,256]{2,1,0:T(8,128)(2,1)S(1)} collective-permute-done((bf16[1,64,256]{2,1,0:T(8,128)(2,1)S(1)}, bf16[1,64,256]{2,1,0:T(8,128)(2,1)S(1)}, u32[]{:S(2)}, u32[]{:S(2)}) %collective-permute-start.29) | collective-permute-done | bytes 32800 | tf_op jit(solution)/shard_map/ppermute | solution.py:15
  125.6 1.2 copy-done.2
  126.8 1.6 fusion.1
  128.4 30.9 %all_to_all.16 = bf16[32,64,256]{2,1,0:T(8,128)(2,1)S(1)} all-to-all(bf16[32,64,256]{2,1,0:T(8,128)(2,1)S(1)} %fusion.1), channel_id=1, replica_groups=mesh['row'=16,'col'=32] {'col'}, dimensions={0} | all-to-all | bytes 2097152 | tf_op jit(solution)/shard_map/all_to_all | solution.py:45
  159.5 1.0 fusion.22
  160.5 1.2 collective-permute-done.30
  161.7 3.3 %collective-permute-start.31 = (bf16[1,64,256]{2,1,0:T(8,128)(2,1)S(1)}, bf16[1,64,256]{2,1,0:T(8,128)(2,1)S(1)}, u32[]{:S(2)}, u32[]{:S(2)}) collective-permute-start(bf16[1,64,256]{2,1,0:T(8,128)(2,1)S(1)} %collective-permute-done.30), channel_id=1, source_target_pairs={{0,32},{32,64},{64,96},{96,128},{128,160},{160,192},{192,224},{224... | collective-permute-start | bytes 98312 | tf_op jit(solution)/shard_map/ppermute | solution.py:13
  165.1 1.0 collective-permute-done.31
  166.1 3.5 %collective-permute-start.32 = (bf16[1,64,256]{2,1,0:T(8,128)(2,1)S(1)}, bf16[1,64,256]{2,1,0:T(8,128)(2,1)}, u32[]{:S(2)}, u32[]{:S(2)}) collective-permute-start(bf16[1,64,256]{2,1,0:T(8,128)(2,1)S(1)} %collective-permute-done.31), channel_id=1, source_target_pairs={{0,32},{32,64},{64,96},{96,128},{128,160},{160,192},{192,224},{224... | collective-permute-start | bytes 98312 | tf_op jit(solution)/shard_map/ppermute | solution.py:13
  169.8 0.8 collective-permute-done.32
  170.6 3.6 %collective-permute-start.33 = (bf16[1,64,256]{2,1,0:T(8,128)(2,1)}, bf16[1,64,256]{2,1,0:T(8,128)(2,1)}, u32[]{:S(2)}, u32[]{:S(2)}) collective-permute-start(bf16[1,64,256]{2,1,0:T(8,128)(2,1)} %collective-permute-done.32), channel_id=1, source_target_pairs={{0,32},{32,64},{64,96},{96,128},{128,160},{160,192},{192,224},{224... | collective-permute-start | bytes 98312 | tf_op jit(solution)/shard_map/ppermute | solution.py:13
  175.7 0.7 copy.36
  177.1 0.7 copy.33
  178.6 2.9 %collective-permute-start.34 = (bf16[1,64,256]{2,1,0:T(8,128)(2,1)}, bf16[1,64,256]{2,1,0:T(8,128)(2,1)S(1)}, u32[]{:S(2)}, u32[]{:S(2)}) collective-permute-start(bf16[1,64,256]{2,1,0:T(8,128)(2,1)} %collective-permute-done.33), channel_id=1, source_target_pairs={{0,32},{32,64},{64,96},{96,128},{128,160},{160,192},{192,224},{224... | collective-permute-start | bytes 98312 | tf_op jit(solution)/shard_map/ppermute | solution.py:13
  181.5 1.0 select_select_fusion.2
  182.5 0.8 collective-permute-done.40
  183.3 3.0 %collective-permute-start.35 = (bf16[1,64,256]{2,1,0:T(8,128)(2,1)S(1)}, bf16[1,64,256]{2,1,0:T(8,128)(2,1)S(1)}, u32[]{:S(2)}, u32[]{:S(2)}) collective-permute-start(bf16[1,64,256]{2,1,0:T(8,128)(2,1)S(1)} %collective-permute-done.34), channel_id=1, source_target_pairs={{0,32},{32,64},{64,96},{96,128},{128,160},{160,192},{192,224},{224... | collective-permute-start | bytes 98312 | tf_op jit(solution)/shard_map/ppermute | solution.py:13
  186.3 2.8 %fusion.9 = f32[32,256,64]{1,2,0:T(8,128)} fusion(bf16[32,128,256]{2,1,0:T(8,128)(2,1)S(1)} %bitcast.153, bf16[6,1,1,32,64,128]{5,4,3,2,1,0:T(8,128)(2,1)} %param.10), kind=kOutput, calls=%fused_computation.34 | convolution fusion | flops 134217728 | bytes 4718592 | tf_op jit(solution)/shard_map/qik,qkn->qin/dot_general | solution.py:26
  189.8 2.9 %collective-permute-start.36 = (bf16[1,64,256]{2,1,0:T(8,128)(2,1)S(1)}, bf16[1,64,256]{2,1,0:T(8,128)(2,1)S(1)}, u32[]{:S(2)}, u32[]{:S(2)}) collective-permute-start(bf16[1,64,256]{2,1,0:T(8,128)(2,1)S(1)} %collective-permute-done.35), channel_id=1, source_target_pairs={{0,32},{32,64},{64,96},{96,128},{128,160},{160,192},{192,224},{224... | collective-permute-start | bytes 98312 | tf_op jit(solution)/shard_map/ppermute | solution.py:13
  193.1 1.3 collective-permute-done.42
  194.3 3.0 %collective-permute-start.37 = (bf16[1,64,256]{2,1,0:T(8,128)(2,1)S(1)}, bf16[1,64,256]{2,1,0:T(8,128)(2,1)S(1)}, u32[]{:S(2)}, u32[]{:S(2)}) collective-permute-start(bf16[1,64,256]{2,1,0:T(8,128)(2,1)S(1)} %collective-permute-done.36), channel_id=1, source_target_pairs={{0,32},{32,64},{64,96},{96,128},{128,160},{160,192},{192,224},{224... | collective-permute-start | bytes 98312 | tf_op jit(solution)/shard_map/ppermute | solution.py:13
  197.3 2.8 %fusion.7 = f32[32,256,64]{1,2,0:T(8,128)} fusion(bf16[32,128,256]{2,1,0:T(8,128)(2,1)S(1)} %bitcast.154, bf16[6,1,1,32,64,128]{5,4,3,2,1,0:T(8,128)(2,1)} %param.10), kind=kOutput, calls=%fused_computation.32 | convolution fusion | flops 134217728 | bytes 4718592 | tf_op jit(solution)/shard_map/qik,qkn->qin/dot_general | solution.py:26
  200.2 0.8 constant_dynamic-update-slice_fusion.43
  201.0 0.8 constant_dynamic-update-slice_fusion.42
  201.8 0.8 constant_dynamic-update-slice_fusion.37
  202.6 2.1 collective-permute-done.44
  206.0 1.2 copy-done
  207.8 1.6 fusion.2
  209.5 30.9 %all_to_all.17 = bf16[32,64,256]{2,1,0:T(8,128)(2,1)S(1)} all-to-all(bf16[32,64,256]{2,1,0:T(8,128)(2,1)S(1)} %fusion.2), channel_id=1, replica_groups=mesh['row'=16,'col'=32] {'col'}, dimensions={0} | all-to-all | bytes 2097152 | tf_op jit(solution)/shard_map/all_to_all | solution.py:45
  240.5 1.0 convolution_bitcast_fusion
  241.5 0.7 maximum_bitcast_fusion
  (169 shorter events, 13.1 us)
Async XLA Ops:
  1.0 4.1 %collective-permute-start = (bf16[1,64,256]{2,1,0:T(8,128)(2,1)S(1)}, bf16[1,64,256]{2,1,0:T(8,128)(2,1)S(1)}, u32[]{:S(2)}, u32[]{:S(2)}) collective-permute-start(bf16[1,64,256]{2,1,0:T(8,128)(2,1)S(1)} %convert_bitcast_fusion), channel_id=1, source_target_pairs={{0,32},{32,64},{64,96},{96,128},{128,160},{160,192},{192,224},{224... | collective-permute-start | bytes 98312 | tf_op jit(solution)/shard_map/ppermute | solution.py:13
  5.1 4.6 %collective-permute-start.1 = (bf16[1,64,256]{2,1,0:T(8,128)(2,1)S(1)}, bf16[1,64,256]{2,1,0:T(8,128)(2,1)S(1)}, u32[]{:S(2)}, u32[]{:S(2)}) collective-permute-start(bf16[1,64,256]{2,1,0:T(8,128)(2,1)S(1)} %collective-permute-done), channel_id=1, source_target_pairs={{0,32},{32,64},{64,96},{96,128},{128,160},{160,192},{192,224},{224... | collective-permute-start | bytes 98312 | tf_op jit(solution)/shard_map/ppermute | solution.py:13
  8.6 4.6 %collective-permute-start.8 = (bf16[1,64,256]{2,1,0:T(8,128)(2,1)S(1)}, bf16[1,64,256]{2,1,0:T(8,128)(2,1)S(1)}, u32[]{:S(2)}, u32[]{:S(2)}) collective-permute-start(bf16[1,64,256]{2,1,0:T(8,128)(2,1)S(1)} %convert_bitcast_fusion), channel_id=1, source_target_pairs={{0,480},{32,0},{64,32},{96,64},{128,96},{160,128},{192,160},{224,1... | collective-permute-start | bytes 98312 | tf_op jit(solution)/shard_map/ppermute | solution.py:15
  9.7 4.6 %collective-permute-start.2 = (bf16[1,64,256]{2,1,0:T(8,128)(2,1)S(1)}, bf16[1,64,256]{2,1,0:T(8,128)(2,1)S(1)}, u32[]{:S(2)}, u32[]{:S(2)}) collective-permute-start(bf16[1,64,256]{2,1,0:T(8,128)(2,1)S(1)} %collective-permute-done.1), channel_id=1, source_target_pairs={{0,32},{32,64},{64,96},{96,128},{128,160},{160,192},{192,224},{224... | collective-permute-start | bytes 98312 | tf_op jit(solution)/shard_map/ppermute | solution.py:13
  13.2 4.6 %collective-permute-start.9 = (bf16[1,64,256]{2,1,0:T(8,128)(2,1)S(1)}, bf16[1,64,256]{2,1,0:T(8,128)(2,1)S(1)}, u32[]{:S(2)}, u32[]{:S(2)}) collective-permute-start(bf16[1,64,256]{2,1,0:T(8,128)(2,1)S(1)} %collective-permute-done.8), channel_id=1, source_target_pairs={{0,480},{32,0},{64,32},{96,64},{128,96},{160,128},{192,160},{224,1... | collective-permute-start | bytes 98312 | tf_op jit(solution)/shard_map/ppermute | solution.py:15
  14.2 4.6 %collective-permute-start.3 = (bf16[1,64,256]{2,1,0:T(8,128)(2,1)S(1)}, bf16[1,64,256]{2,1,0:T(8,128)(2,1)S(1)}, u32[]{:S(2)}, u32[]{:S(2)}) collective-permute-start(bf16[1,64,256]{2,1,0:T(8,128)(2,1)S(1)} %collective-permute-done.2), channel_id=1, source_target_pairs={{0,32},{32,64},{64,96},{96,128},{128,160},{160,192},{192,224},{224... | collective-permute-start | bytes 98312 | tf_op jit(solution)/shard_map/ppermute | solution.py:13
  17.7 4.6 %collective-permute-start.10 = (bf16[1,64,256]{2,1,0:T(8,128)(2,1)S(1)}, bf16[1,64,256]{2,1,0:T(8,128)(2,1)S(1)}, u32[]{:S(2)}, u32[]{:S(2)}) collective-permute-start(bf16[1,64,256]{2,1,0:T(8,128)(2,1)S(1)} %collective-permute-done.9), channel_id=1, source_target_pairs={{0,480},{32,0},{64,32},{96,64},{128,96},{160,128},{192,160},{224,1... | collective-permute-start | bytes 98312 | tf_op jit(solution)/shard_map/ppermute | solution.py:15
  18.8 4.6 %collective-permute-start.4 = (bf16[1,64,256]{2,1,0:T(8,128)(2,1)S(1)}, bf16[1,64,256]{2,1,0:T(8,128)(2,1)S(1)}, u32[]{:S(2)}, u32[]{:S(2)}) collective-permute-start(bf16[1,64,256]{2,1,0:T(8,128)(2,1)S(1)} %collective-permute-done.3), channel_id=1, source_target_pairs={{0,32},{32,64},{64,96},{96,128},{128,160},{160,192},{192,224},{224... | collective-permute-start | bytes 98312 | tf_op jit(solution)/shard_map/ppermute | solution.py:13
  22.3 5.9 %collective-permute-start.11 = (bf16[1,64,256]{2,1,0:T(8,128)(2,1)S(1)}, bf16[1,64,256]{2,1,0:T(8,128)(2,1)S(1)}, u32[]{:S(2)}, u32[]{:S(2)}) collective-permute-start(bf16[1,64,256]{2,1,0:T(8,128)(2,1)S(1)} %collective-permute-done.10), channel_id=1, source_target_pairs={{0,480},{32,0},{64,32},{96,64},{128,96},{160,128},{192,160},{224,1... | collective-permute-start | bytes 98312 | tf_op jit(solution)/shard_map/ppermute | solution.py:15
  23.3 4.9 %collective-permute-start.5 = (bf16[1,64,256]{2,1,0:T(8,128)(2,1)S(1)}, bf16[1,64,256]{2,1,0:T(8,128)(2,1)S(1)}, u32[]{:S(2)}, u32[]{:S(2)}) collective-permute-start(bf16[1,64,256]{2,1,0:T(8,128)(2,1)S(1)} %collective-permute-done.4), channel_id=1, source_target_pairs={{0,32},{32,64},{64,96},{96,128},{128,160},{160,192},{192,224},{224... | collective-permute-start | bytes 98312 | tf_op jit(solution)/shard_map/ppermute | solution.py:13
  28.2 4.8 %collective-permute-start.12 = (bf16[1,64,256]{2,1,0:T(8,128)(2,1)S(1)}, bf16[1,64,256]{2,1,0:T(8,128)(2,1)S(1)}, u32[]{:S(2)}, u32[]{:S(2)}) collective-permute-start(bf16[1,64,256]{2,1,0:T(8,128)(2,1)S(1)} %collective-permute-done.11), channel_id=1, source_target_pairs={{0,480},{32,0},{64,32},{96,64},{128,96},{160,128},{192,160},{224,1... | collective-permute-start | bytes 98312 | tf_op jit(solution)/shard_map/ppermute | solution.py:15
  28.2 4.8 %collective-permute-start.6 = (bf16[1,64,256]{2,1,0:T(8,128)(2,1)S(1)}, bf16[1,64,256]{2,1,0:T(8,128)(2,1)S(1)}, u32[]{:S(2)}, u32[]{:S(2)}) collective-permute-start(bf16[1,64,256]{2,1,0:T(8,128)(2,1)S(1)} %collective-permute-done.5), channel_id=1, source_target_pairs={{0,32},{32,64},{64,96},{96,128},{128,160},{160,192},{192,224},{224... | collective-permute-start | bytes 98312 | tf_op jit(solution)/shard_map/ppermute | solution.py:13
  32.9 4.6 %collective-permute-start.13 = (bf16[1,64,256]{2,1,0:T(8,128)(2,1)S(1)}, bf16[1,64,256]{2,1,0:T(8,128)(2,1)S(1)}, u32[]{:S(2)}, u32[]{:S(2)}) collective-permute-start(bf16[1,64,256]{2,1,0:T(8,128)(2,1)S(1)} %collective-permute-done.12), channel_id=1, source_target_pairs={{0,480},{32,0},{64,32},{96,64},{128,96},{160,128},{192,160},{224,1... | collective-permute-start | bytes 98312 | tf_op jit(solution)/shard_map/ppermute | solution.py:15
  33.0 4.5 %collective-permute-start.7 = (bf16[1,64,256]{2,1,0:T(8,128)(2,1)S(1)}, bf16[1,64,256]{2,1,0:T(8,128)(2,1)S(1)}, u32[]{:S(2)}, u32[]{:S(2)}) collective-permute-start(bf16[1,64,256]{2,1,0:T(8,128)(2,1)S(1)} %collective-permute-done.6), channel_id=1, source_target_pairs={{0,32},{32,64},{64,96},{96,128},{128,160},{160,192},{192,224},{224... | collective-permute-start | bytes 98312 | tf_op jit(solution)/shard_map/ppermute | solution.py:13
  37.5 4.6 %collective-permute-start.14 = (bf16[1,64,256]{2,1,0:T(8,128)(2,1)S(1)}, bf16[1,64,256]{2,1,0:T(8,128)(2,1)S(1)}, u32[]{:S(2)}, u32[]{:S(2)}) collective-permute-start(bf16[1,64,256]{2,1,0:T(8,128)(2,1)S(1)} %collective-permute-done.13), channel_id=1, source_target_pairs={{0,480},{32,0},{64,32},{96,64},{128,96},{160,128},{192,160},{224,1... | collective-permute-start | bytes 98312 | tf_op jit(solution)/shard_map/ppermute | solution.py:15
  44.8 39.3 %copy-start.3 = (bf16[4,1,1,64,256]{4,3,2,1,0:T(8,128)(2,1)S(1)}, bf16[4,1,1,64,256]{4,3,2,1,0:T(8,128)(2,1)}, u32[]{:S(2)}) copy-start(bf16[4,1,1,64,256]{4,3,2,1,0:T(8,128)(2,1)} %param.8) | copy-start | bytes 393220
  85.1 1.2 collective-permute-start.15
  86.3 4.4 %collective-permute-start.16 = (bf16[1,64,256]{2,1,0:T(8,128)(2,1)S(1)}, bf16[1,64,256]{2,1,0:T(8,128)(2,1)S(1)}, u32[]{:S(2)}, u32[]{:S(2)}) collective-permute-start(bf16[1,64,256]{2,1,0:T(8,128)(2,1)S(1)} %collective-permute-done.15), channel_id=1, source_target_pairs={{0,32},{32,64},{64,96},{96,128},{128,160},{160,192},{192,224},{224... | collective-permute-start | bytes 98312 | tf_op jit(solution)/shard_map/ppermute | solution.py:13
  89.6 4.6 %collective-permute-start.23 = (bf16[1,64,256]{2,1,0:T(8,128)(2,1)S(1)}, bf16[1,64,256]{2,1,0:T(8,128)(2,1)S(1)}, u32[]{:S(2)}, u32[]{:S(2)}) collective-permute-start(bf16[1,64,256]{2,1,0:T(8,128)(2,1)S(1)} %fusion.29), channel_id=1, source_target_pairs={{0,480},{32,0},{64,32},{96,64},{128,96},{160,128},{192,160},{224,1... | collective-permute-start | bytes 98312 | tf_op jit(solution)/shard_map/ppermute | solution.py:15
  90.7 4.6 %collective-permute-start.17 = (bf16[1,64,256]{2,1,0:T(8,128)(2,1)S(1)}, bf16[1,64,256]{2,1,0:T(8,128)(2,1)S(1)}, u32[]{:S(2)}, u32[]{:S(2)}) collective-permute-start(bf16[1,64,256]{2,1,0:T(8,128)(2,1)S(1)} %collective-permute-done.16), channel_id=1, source_target_pairs={{0,32},{32,64},{64,96},{96,128},{128,160},{160,192},{192,224},{224... | collective-permute-start | bytes 98312 | tf_op jit(solution)/shard_map/ppermute | solution.py:13
  94.2 4.9 %collective-permute-start.24 = (bf16[1,64,256]{2,1,0:T(8,128)(2,1)S(1)}, bf16[1,64,256]{2,1,0:T(8,128)(2,1)S(1)}, u32[]{:S(2)}, u32[]{:S(2)}) collective-permute-start(bf16[1,64,256]{2,1,0:T(8,128)(2,1)S(1)} %collective-permute-done.23), channel_id=1, source_target_pairs={{0,480},{32,0},{64,32},{96,64},{128,96},{160,128},{192,160},{224,1... | collective-permute-start | bytes 98312 | tf_op jit(solution)/shard_map/ppermute | solution.py:15
  95.2 4.6 %collective-permute-start.18 = (bf16[1,64,256]{2,1,0:T(8,128)(2,1)S(1)}, bf16[1,64,256]{2,1,0:T(8,128)(2,1)S(1)}, u32[]{:S(2)}, u32[]{:S(2)}) collective-permute-start(bf16[1,64,256]{2,1,0:T(8,128)(2,1)S(1)} %collective-permute-done.17), channel_id=1, source_target_pairs={{0,32},{32,64},{64,96},{96,128},{128,160},{160,192},{192,224},{224... | collective-permute-start | bytes 98312 | tf_op jit(solution)/shard_map/ppermute | solution.py:13
  99.1 4.6 %collective-permute-start.25 = (bf16[1,64,256]{2,1,0:T(8,128)(2,1)S(1)}, bf16[1,64,256]{2,1,0:T(8,128)(2,1)S(1)}, u32[]{:S(2)}, u32[]{:S(2)}) collective-permute-start(bf16[1,64,256]{2,1,0:T(8,128)(2,1)S(1)} %collective-permute-done.24), channel_id=1, source_target_pairs={{0,480},{32,0},{64,32},{96,64},{128,96},{160,128},{192,160},{224,1... | collective-permute-start | bytes 98312 | tf_op jit(solution)/shard_map/ppermute | solution.py:15
  99.8 4.6 %collective-permute-start.19 = (bf16[1,64,256]{2,1,0:T(8,128)(2,1)S(1)}, bf16[1,64,256]{2,1,0:T(8,128)(2,1)S(1)}, u32[]{:S(2)}, u32[]{:S(2)}) collective-permute-start(bf16[1,64,256]{2,1,0:T(8,128)(2,1)S(1)} %collective-permute-done.18), channel_id=1, source_target_pairs={{0,32},{32,64},{64,96},{96,128},{128,160},{160,192},{192,224},{224... | collective-permute-start | bytes 98312 | tf_op jit(solution)/shard_map/ppermute | solution.py:13
  103.7 5.2 %collective-permute-start.26 = (bf16[1,64,256]{2,1,0:T(8,128)(2,1)S(1)}, bf16[1,64,256]{2,1,0:T(8,128)(2,1)S(1)}, u32[]{:S(2)}, u32[]{:S(2)}) collective-permute-start(bf16[1,64,256]{2,1,0:T(8,128)(2,1)S(1)} %collective-permute-done.25), channel_id=1, source_target_pairs={{0,480},{32,0},{64,32},{96,64},{128,96},{160,128},{192,160},{224,1... | collective-permute-start | bytes 98312 | tf_op jit(solution)/shard_map/ppermute | solution.py:15
  104.3 4.7 %collective-permute-start.20 = (bf16[1,64,256]{2,1,0:T(8,128)(2,1)S(1)}, bf16[1,64,256]{2,1,0:T(8,128)(2,1)S(1)}, u32[]{:S(2)}, u32[]{:S(2)}) collective-permute-start(bf16[1,64,256]{2,1,0:T(8,128)(2,1)S(1)} %collective-permute-done.19), channel_id=1, source_target_pairs={{0,32},{32,64},{64,96},{96,128},{128,160},{160,192},{192,224},{224... | collective-permute-start | bytes 98312 | tf_op jit(solution)/shard_map/ppermute | solution.py:13
  109.0 4.6 %collective-permute-start.27 = (bf16[1,64,256]{2,1,0:T(8,128)(2,1)S(1)}, bf16[1,64,256]{2,1,0:T(8,128)(2,1)S(1)}, u32[]{:S(2)}, u32[]{:S(2)}) collective-permute-start(bf16[1,64,256]{2,1,0:T(8,128)(2,1)S(1)} %collective-permute-done.26), channel_id=1, source_target_pairs={{0,480},{32,0},{64,32},{96,64},{128,96},{160,128},{192,160},{224,1... | collective-permute-start | bytes 98312 | tf_op jit(solution)/shard_map/ppermute | solution.py:15
  109.0 4.5 %collective-permute-start.21 = (bf16[1,64,256]{2,1,0:T(8,128)(2,1)S(1)}, bf16[1,64,256]{2,1,0:T(8,128)(2,1)S(1)}, u32[]{:S(2)}, u32[]{:S(2)}) collective-permute-start(bf16[1,64,256]{2,1,0:T(8,128)(2,1)S(1)} %collective-permute-done.20), channel_id=1, source_target_pairs={{0,32},{32,64},{64,96},{96,128},{128,160},{160,192},{192,224},{224... | collective-permute-start | bytes 98312 | tf_op jit(solution)/shard_map/ppermute | solution.py:13
  113.5 6.2 %collective-permute-start.28 = (bf16[1,64,256]{2,1,0:T(8,128)(2,1)S(1)}, bf16[1,64,256]{2,1,0:T(8,128)(2,1)S(1)}, u32[]{:S(2)}, u32[]{:S(2)}) collective-permute-start(bf16[1,64,256]{2,1,0:T(8,128)(2,1)S(1)} %collective-permute-done.27), channel_id=1, source_target_pairs={{0,480},{32,0},{64,32},{96,64},{128,96},{160,128},{192,160},{224,1... | collective-permute-start | bytes 98312 | tf_op jit(solution)/shard_map/ppermute | solution.py:15
  113.5 6.2 %collective-permute-start.22 = (bf16[1,64,256]{2,1,0:T(8,128)(2,1)S(1)}, bf16[1,64,256]{2,1,0:T(8,128)(2,1)S(1)}, u32[]{:S(2)}, u32[]{:S(2)}) collective-permute-start(bf16[1,64,256]{2,1,0:T(8,128)(2,1)S(1)} %collective-permute-done.21), channel_id=1, source_target_pairs={{0,32},{32,64},{64,96},{96,128},{128,160},{160,192},{192,224},{224... | collective-permute-start | bytes 98312 | tf_op jit(solution)/shard_map/ppermute | solution.py:13
  119.8 4.6 %collective-permute-start.29 = (bf16[1,64,256]{2,1,0:T(8,128)(2,1)S(1)}, bf16[1,64,256]{2,1,0:T(8,128)(2,1)S(1)}, u32[]{:S(2)}, u32[]{:S(2)}) collective-permute-start(bf16[1,64,256]{2,1,0:T(8,128)(2,1)S(1)} %collective-permute-done.28), channel_id=1, source_target_pairs={{0,480},{32,0},{64,32},{96,64},{128,96},{160,128},{192,160},{224,1... | collective-permute-start | bytes 98312 | tf_op jit(solution)/shard_map/ppermute | solution.py:15
  125.2 1.6 copy-start.2
  128.4 45.9 %copy-start.11 = (pred[32,2]{0,1:T(4,128)(4,1)S(1)}, pred[32,2]{0,1:T(4,128)(4,1)}, u32[]{:S(2)}) copy-start(pred[32,2]{0,1:T(4,128)(4,1)} %get-tuple-element.33) | copy-start | bytes 196
  128.4 46.0 %copy-start.14 = (pred[32,2]{0,1:T(4,128)(4,1)S(1)}, pred[32,2]{0,1:T(4,128)(4,1)}, u32[]{:S(2)}) copy-start(pred[32,2]{0,1:T(4,128)(4,1)} %get-tuple-element.24) | copy-start | bytes 196
  128.4 46.7 %copy-start.10 = (pred[32,2]{0,1:T(4,128)(4,1)S(1)}, pred[32,2]{0,1:T(4,128)(4,1)}, u32[]{:S(2)}) copy-start(pred[32,2]{0,1:T(4,128)(4,1)} %get-tuple-element.6) | copy-start | bytes 196
  128.4 47.3 %copy-start.13 = (pred[32,2]{0,1:T(4,128)(4,1)S(1)}, pred[32,2]{0,1:T(4,128)(4,1)}, u32[]{:S(2)}) copy-start(pred[32,2]{0,1:T(4,128)(4,1)} %get-tuple-element.19) | copy-start | bytes 196
  128.4 48.0 %copy-start.9 = (pred[32,2]{0,1:T(4,128)(4,1)S(1)}, pred[32,2]{0,1:T(4,128)(4,1)}, u32[]{:S(2)}) copy-start(pred[32,2]{0,1:T(4,128)(4,1)} %get-tuple-element.31) | copy-start | bytes 196
  128.4 48.7 %copy-start.12 = (pred[32,2]{0,1:T(4,128)(4,1)S(1)}, pred[32,2]{0,1:T(4,128)(4,1)}, u32[]{:S(2)}) copy-start(pred[32,2]{0,1:T(4,128)(4,1)} %get-tuple-element.20) | copy-start | bytes 196
  160.5 1.2 collective-permute-start.30
  161.7 4.4 %collective-permute-start.31 = (bf16[1,64,256]{2,1,0:T(8,128)(2,1)S(1)}, bf16[1,64,256]{2,1,0:T(8,128)(2,1)S(1)}, u32[]{:S(2)}, u32[]{:S(2)}) collective-permute-start(bf16[1,64,256]{2,1,0:T(8,128)(2,1)S(1)} %collective-permute-done.30), channel_id=1, source_target_pairs={{0,32},{32,64},{64,96},{96,128},{128,160},{160,192},{192,224},{224... | collective-permute-start | bytes 98312 | tf_op jit(solution)/shard_map/ppermute | solution.py:13
  165.1 4.7 %collective-permute-start.38 = (bf16[1,64,256]{2,1,0:T(8,128)(2,1)S(1)}, bf16[1,64,256]{2,1,0:T(8,128)(2,1)S(1)}, u32[]{:S(2)}, u32[]{:S(2)}) collective-permute-start(bf16[1,64,256]{2,1,0:T(8,128)(2,1)S(1)} %fusion.30), channel_id=1, source_target_pairs={{0,480},{32,0},{64,32},{96,64},{128,96},{160,128},{192,160},{224,1... | collective-permute-start | bytes 98312 | tf_op jit(solution)/shard_map/ppermute | solution.py:15
  166.1 11.7 %copy-start.4 = (bf16[1,64,256]{2,1,0:T(8,128)(2,1)}, bf16[1,64,256]{2,1,0:T(8,128)(2,1)S(1)}, u32[]{:S(2)}) copy-start(bf16[1,64,256]{2,1,0:T(8,128)(2,1)S(1)} %collective-permute-done.31) | copy-start | bytes 98308
  166.1 4.6 %collective-permute-start.32 = (bf16[1,64,256]{2,1,0:T(8,128)(2,1)S(1)}, bf16[1,64,256]{2,1,0:T(8,128)(2,1)}, u32[]{:S(2)}, u32[]{:S(2)}) collective-permute-start(bf16[1,64,256]{2,1,0:T(8,128)(2,1)S(1)} %collective-permute-done.31), channel_id=1, source_target_pairs={{0,32},{32,64},{64,96},{96,128},{128,160},{160,192},{192,224},{224... | collective-permute-start | bytes 98312 | tf_op jit(solution)/shard_map/ppermute | solution.py:13
  169.8 8.7 %collective-permute-start.39 = (bf16[1,64,256]{2,1,0:T(8,128)(2,1)S(1)}, bf16[1,64,256]{2,1,0:T(8,128)(2,1)}, u32[]{:S(2)}, u32[]{:S(2)}) collective-permute-start(bf16[1,64,256]{2,1,0:T(8,128)(2,1)S(1)} %collective-permute-done.38), channel_id=1, source_target_pairs={{0,480},{32,0},{64,32},{96,64},{128,96},{160,128},{192,160},{224,1... | collective-permute-start | bytes 98312 | tf_op jit(solution)/shard_map/ppermute | solution.py:15
  170.6 7.9 %collective-permute-start.33 = (bf16[1,64,256]{2,1,0:T(8,128)(2,1)}, bf16[1,64,256]{2,1,0:T(8,128)(2,1)}, u32[]{:S(2)}, u32[]{:S(2)}) collective-permute-start(bf16[1,64,256]{2,1,0:T(8,128)(2,1)} %collective-permute-done.32), channel_id=1, source_target_pairs={{0,32},{32,64},{64,96},{96,128},{128,160},{160,192},{192,224},{224... | collective-permute-start | bytes 98312 | tf_op jit(solution)/shard_map/ppermute | solution.py:13
  178.5 4.8 %collective-permute-start.40 = (bf16[1,64,256]{2,1,0:T(8,128)(2,1)}, bf16[1,64,256]{2,1,0:T(8,128)(2,1)S(1)}, u32[]{:S(2)}, u32[]{:S(2)}) collective-permute-start(bf16[1,64,256]{2,1,0:T(8,128)(2,1)} %collective-permute-done.39), channel_id=1, source_target_pairs={{0,480},{32,0},{64,32},{96,64},{128,96},{160,128},{192,160},{224,1... | collective-permute-start | bytes 98312 | tf_op jit(solution)/shard_map/ppermute | solution.py:15
  178.6 4.7 %collective-permute-start.34 = (bf16[1,64,256]{2,1,0:T(8,128)(2,1)}, bf16[1,64,256]{2,1,0:T(8,128)(2,1)S(1)}, u32[]{:S(2)}, u32[]{:S(2)}) collective-permute-start(bf16[1,64,256]{2,1,0:T(8,128)(2,1)} %collective-permute-done.33), channel_id=1, source_target_pairs={{0,32},{32,64},{64,96},{96,128},{128,160},{160,192},{192,224},{224... | collective-permute-start | bytes 98312 | tf_op jit(solution)/shard_map/ppermute | solution.py:13
  183.3 6.5 %collective-permute-start.41 = (bf16[1,64,256]{2,1,0:T(8,128)(2,1)S(1)}, bf16[1,64,256]{2,1,0:T(8,128)(2,1)S(1)}, u32[]{:S(2)}, u32[]{:S(2)}) collective-permute-start(bf16[1,64,256]{2,1,0:T(8,128)(2,1)S(1)} %collective-permute-done.40), channel_id=1, source_target_pairs={{0,480},{32,0},{64,32},{96,64},{128,96},{160,128},{192,160},{224,1... | collective-permute-start | bytes 98312 | tf_op jit(solution)/shard_map/ppermute | solution.py:15
  183.3 6.5 %collective-permute-start.35 = (bf16[1,64,256]{2,1,0:T(8,128)(2,1)S(1)}, bf16[1,64,256]{2,1,0:T(8,128)(2,1)S(1)}, u32[]{:S(2)}, u32[]{:S(2)}) collective-permute-start(bf16[1,64,256]{2,1,0:T(8,128)(2,1)S(1)} %collective-permute-done.34), channel_id=1, source_target_pairs={{0,32},{32,64},{64,96},{96,128},{128,160},{160,192},{192,224},{224... | collective-permute-start | bytes 98312 | tf_op jit(solution)/shard_map/ppermute | solution.py:13
  189.1 3.7 %copy-start.7 = (pred[32,2]{1,0:T(8,128)(4,1)S(1)}, pred[32,2]{1,0:T(8,128)(4,1)}, u32[]{:S(2)}) copy-start(pred[32,2]{1,0:T(8,128)(4,1)} %copy.37) | copy-start | bytes 196
  189.1 3.7 %copy-start.8 = (pred[32,2]{1,0:T(8,128)(4,1)S(1)}, pred[32,2]{1,0:T(8,128)(4,1)}, u32[]{:S(2)}) copy-start(pred[32,2]{1,0:T(8,128)(4,1)} %copy.36) | copy-start | bytes 196
  189.8 4.6 %collective-permute-start.42 = (bf16[1,64,256]{2,1,0:T(8,128)(2,1)S(1)}, bf16[1,64,256]{2,1,0:T(8,128)(2,1)S(1)}, u32[]{:S(2)}, u32[]{:S(2)}) collective-permute-start(bf16[1,64,256]{2,1,0:T(8,128)(2,1)S(1)} %collective-permute-done.41), channel_id=1, source_target_pairs={{0,480},{32,0},{64,32},{96,64},{128,96},{160,128},{192,160},{224,1... | collective-permute-start | bytes 98312 | tf_op jit(solution)/shard_map/ppermute | solution.py:15
  189.8 4.5 %collective-permute-start.36 = (bf16[1,64,256]{2,1,0:T(8,128)(2,1)S(1)}, bf16[1,64,256]{2,1,0:T(8,128)(2,1)S(1)}, u32[]{:S(2)}, u32[]{:S(2)}) collective-permute-start(bf16[1,64,256]{2,1,0:T(8,128)(2,1)S(1)} %collective-permute-done.35), channel_id=1, source_target_pairs={{0,32},{32,64},{64,96},{96,128},{128,160},{160,192},{192,224},{224... | collective-permute-start | bytes 98312 | tf_op jit(solution)/shard_map/ppermute | solution.py:13
  194.3 5.8 %collective-permute-start.43 = (bf16[1,64,256]{2,1,0:T(8,128)(2,1)S(1)}, bf16[1,64,256]{2,1,0:T(8,128)(2,1)S(1)}, u32[]{:S(2)}, u32[]{:S(2)}) collective-permute-start(bf16[1,64,256]{2,1,0:T(8,128)(2,1)S(1)} %collective-permute-done.42), channel_id=1, source_target_pairs={{0,480},{32,0},{64,32},{96,64},{128,96},{160,128},{192,160},{224,1... | collective-permute-start | bytes 98312 | tf_op jit(solution)/shard_map/ppermute | solution.py:15
  194.3 5.8 %collective-permute-start.37 = (bf16[1,64,256]{2,1,0:T(8,128)(2,1)S(1)}, bf16[1,64,256]{2,1,0:T(8,128)(2,1)S(1)}, u32[]{:S(2)}, u32[]{:S(2)}) collective-permute-start(bf16[1,64,256]{2,1,0:T(8,128)(2,1)S(1)} %collective-permute-done.36), channel_id=1, source_target_pairs={{0,32},{32,64},{64,96},{96,128},{128,160},{160,192},{192,224},{224... | collective-permute-start | bytes 98312 | tf_op jit(solution)/shard_map/ppermute | solution.py:13
  197.3 4.4 %copy-start.5 = (bf16[1,64,256]{2,1,0:T(8,128)(2,1)S(1)}, bf16[1,64,256]{2,1,0:T(8,128)(2,1)}, u32[]{:S(2)}) copy-start(bf16[1,64,256]{2,1,0:T(8,128)(2,1)} %copy-done.4) | copy-start | bytes 98308
  200.1 4.6 %collective-permute-start.44 = (bf16[1,64,256]{2,1,0:T(8,128)(2,1)S(1)}, bf16[1,64,256]{2,1,0:T(8,128)(2,1)S(1)}, u32[]{:S(2)}, u32[]{:S(2)}) collective-permute-start(bf16[1,64,256]{2,1,0:T(8,128)(2,1)S(1)} %collective-permute-done.43), channel_id=1, source_target_pairs={{0,480},{32,0},{64,32},{96,64},{128,96},{160,128},{192,160},{224,1... | collective-permute-start | bytes 98312 | tf_op jit(solution)/shard_map/ppermute | solution.py:15
  204.9 0.7 copy-start.6
  205.6 1.6 copy-start
  205.6 2.2 copy-start.1
